TPU v7x, 32 devices: a whole 2x2x4 slice. The times are simulated.
32 devices in a mesh: seq: 16 (over z, x, core), dp: 2 (over y).
Axes of the slice: x: 2, y: 2, z: 4, core: 2. Of those that a mesh axis runs over, the one named last changes fastest.
Arguments:
- queries: bfloat16 [2, 1024, 2048], P(None, 'seq', 'dp'), may hold values from -10 to 10
- key_rows: bfloat16 [2, 1024, 2048], P(None, 'seq', 'dp'), may hold values from -10 to 10
- value_rows: bfloat16 [2, 1024, 2048], P(None, 'seq', 'dp'), may hold values from -6 to 6
- query_tangent: bfloat16 [2, 1024, 2048], P(None, 'seq', 'dp'), may hold values from -6 to 6
- key_tangent: bfloat16 [2, 1024, 2048], P(None, 'seq', 'dp'), may hold values from -6 to 6
- out_adjoint: bfloat16 [2, 1024, 2048], P(None, 'seq', 'dp'), may hold values from -6 to 6
Outputs:
- query_product: bfloat16 [2, 1024, 2048], P(None, 'seq', 'dp')
- key_product: bfloat16 [2, 1024, 2048], P(None, 'seq', 'dp')
- value_product: bfloat16 [2, 1024, 2048], P(None, 'seq', 'dp')
- curvature: float32 [2, 16], replicated
All inputs are finite; a program needn't handle non-finite values.
Results may differ from a plain program's by a relative error of at most 0.0051.
Values may be sent and summed in bfloat16 or wider, within the bound.
A program may use at most 64 MiB of HBM per device.

v0:
```python
import jax
import jax.numpy as jnp
from jax import lax
from jax.sharding import PartitionSpec as P

HEAD_DIM = 128


def inner_rows(left, right):
    return lax.dot_general(
        left, right, (((1,), (1,)), ((), ())), preferred_element_type=jnp.float32
    )


def inner_cols(left, right):
    return lax.dot_general(
        left, right, (((0,), (0,)), ((), ())), preferred_element_type=jnp.float32
    )


def score_block(query, keyset, tquery, tkey, start, block_size):
    factor = HEAD_DIM ** (-0.5)
    stop = start + block_size
    query_block = query[start:stop]
    key_block = keyset[:stop]
    scores = factor * inner_rows(query_block, key_block)
    row_index = start + jnp.arange(block_size)[:, None]
    col_index = jnp.arange(stop)[None, :]
    scores = jnp.where(row_index >= col_index, scores, -jnp.inf)
    top_score = jnp.max(scores, axis=1, keepdims=True)
    weights = jnp.exp(scores - top_score)
    probs = weights / jnp.sum(weights, axis=1, keepdims=True)
    tangent_scores = factor * (
        inner_rows(tquery[start:stop], key_block) + inner_rows(query_block, tkey[:stop])
    )
    mean_tangent = jnp.sum(probs * tangent_scores, axis=1, keepdims=True)
    tangent_probs = probs * (tangent_scores - mean_tangent)
    return (probs, tangent_probs)


def head_work(tensors):
    query, keyset, values_in, tquery, tkey, adjoint = tensors
    factor = HEAD_DIM ** (-0.5)
    length = query.shape[0]
    block_size = min(512, length)
    key_hvp = jnp.zeros((length, HEAD_DIM), jnp.float32)
    value_hvp = jnp.zeros((length, HEAD_DIM), jnp.float32)
    query_parts = []
    for number in range(length // block_size):
        start = number * block_size
        stop = start + block_size
        probs, tangent_probs = score_block(query, keyset, tquery, tkey, start, block_size)
        adj_block = adjoint[start:stop]
        grad_probs = inner_rows(adj_block, values_in[:stop])
        delta = jnp.sum(probs * grad_probs, axis=1, keepdims=True)
        centered = grad_probs - delta
        grad_scores = probs * centered
        tangent_delta = jnp.sum(tangent_probs * grad_probs, axis=1, keepdims=True)
        second_scores = tangent_probs * centered - probs * tangent_delta
        tprob_low = tangent_probs.astype(jnp.bfloat16)
        gscore_low = grad_scores.astype(jnp.bfloat16)
        second_low = second_scores.astype(jnp.bfloat16)
        value_hvp = value_hvp.at[:stop].add(inner_cols(tprob_low, adj_block))
        query_parts.append(
            factor
            * (
                jnp.dot(second_low, keyset[:stop], preferred_element_type=jnp.float32)
                + jnp.dot(gscore_low, tkey[:stop], preferred_element_type=jnp.float32)
            )
        )
        key_hvp = key_hvp.at[:stop].add(
            factor
            * (
                inner_cols(second_low, query[start:stop])
                + inner_cols(gscore_low, tquery[start:stop])
            )
        )
    query_hvp = jnp.concatenate(query_parts, axis=0)
    kappa = jnp.sum(tquery.astype(jnp.float32) * query_hvp) + jnp.sum(
        tkey.astype(jnp.float32) * key_hvp
    )
    return (query_hvp, key_hvp, value_hvp, kappa)


def local(queries, key_rows, value_rows, query_tangent, key_tangent, out_adjoint):
    batch_count = queries.shape[0]
    tokens_here = queries.shape[1]
    local_heads = queries.shape[2] // HEAD_DIM

    def to_items(tensor):
        shaped = tensor.reshape(batch_count, tokens_here, local_heads, HEAD_DIM)
        return jnp.transpose(shaped, (0, 2, 1, 3)).reshape(
            batch_count * local_heads, tokens_here, HEAD_DIM
        )

    parts = (
        lax.all_to_all(to_items(queries), "seq", split_axis=0, concat_axis=1, tiled=True),
        lax.all_to_all(to_items(key_rows), "seq", split_axis=0, concat_axis=1, tiled=True),
        lax.all_to_all(to_items(value_rows), "seq", split_axis=0, concat_axis=1, tiled=True),
        lax.all_to_all(to_items(query_tangent), "seq", split_axis=0, concat_axis=1, tiled=True),
        lax.all_to_all(to_items(key_tangent), "seq", split_axis=0, concat_axis=1, tiled=True),
        lax.all_to_all(to_items(out_adjoint), "seq", split_axis=0, concat_axis=1, tiled=True),
    )
    item_count = parts[0].shape[0]
    item = 0
    tensors = tuple((part[item] for part in parts))
    query_hvp, key_hvp, value_hvp, kappa = head_work(tensors)
    query_items = [query_hvp.astype(jnp.bfloat16)]
    key_items = [key_hvp.astype(jnp.bfloat16)]
    value_items = [value_hvp.astype(jnp.bfloat16)]
    kappas = [kappa]
    returned = (
        lax.all_to_all(jnp.stack(query_items), "seq", split_axis=1, concat_axis=0, tiled=True),
        lax.all_to_all(jnp.stack(key_items), "seq", split_axis=1, concat_axis=0, tiled=True),
        lax.all_to_all(jnp.stack(value_items), "seq", split_axis=1, concat_axis=0, tiled=True),
    )

    def to_tokens(tensor):
        shaped = tensor.reshape(batch_count, local_heads, tokens_here, HEAD_DIM)
        return jnp.transpose(shaped, (0, 2, 1, 3)).reshape(
            batch_count, tokens_here, local_heads * HEAD_DIM
        )

    outputs = tuple((to_tokens(piece) for piece in returned))
    heads_total = local_heads * lax.axis_size("dp")
    batch_index = jnp.arange(batch_count)[:, None]
    head_index = jnp.arange(heads_total)[None, :]
    item = 0
    global_item = lax.axis_index("seq") * item_count + item
    batch_here = global_item // local_heads
    head_here = lax.axis_index("dp") * local_heads + global_item % local_heads
    hit = jnp.logical_and(batch_index == batch_here, head_index == head_here)
    board = jnp.where(hit, kappas[item], 0.0)
    curvature = lax.psum(board, ("seq", "dp"))
    return (outputs[0], outputs[1], outputs[2], curvature)


def solution(mesh):
    return jax.shard_map(
        local,
        mesh=mesh,
        in_specs=(
            P(None, "seq", "dp"),
            P(None, "seq", "dp"),
            P(None, "seq", "dp"),
            P(None, "seq", "dp"),
            P(None, "seq", "dp"),
            P(None, "seq", "dp"),
        ),
        out_specs=(P(None, "seq", "dp"), P(None, "seq", "dp"), P(None, "seq", "dp"), P()),
        check_vma=False,
    )
```

profile of v0, /device:TPU:0, one launch (start us, length us, event | category | flops | bytes accessed | tf_op | source)
XLA Modules:
  0.0 181.6 jit_solution(2033972565623164572)
XLA Ops:
  0.7 1.1 copy.68
  1.8 0.8 copy.50
  2.5 7.4 %all-to-all-start = ((bf16[16,64,128]{2,1,0:T(8,128)(2,1)}), bf16[16,64,128]{2,1,0:T(8,128)(2,1)S(1)}, u32[]{:S(2)}, u32[]{:S(2)}) async-start(bf16[16,64,128]{2,1,0:T(8,128)(2,1)} %bitcast.1), calls=%async_computation | async-start | bytes 524288 | tf_op jit(solution)/shard_map/all_to_all | solution.py:97
  10.0 0.8 copy.51
  10.9 9.0 %all-to-all-done = bf16[16,64,128]{2,1,0:T(8,128)(2,1)S(1)} async-done(((bf16[16,64,128]{2,1,0:T(8,128)(2,1)}), bf16[16,64,128]{2,1,0:T(8,128)(2,1)S(1)}, u32[]{:S(2)}, u32[]{:S(2)}) %all-to-all-start) | async-done | bytes 262176 | tf_op jit(solution)/shard_map/all_to_all | solution.py:97
  19.9 3.5 %all-to-all-start.1 = ((bf16[16,64,128]{2,1,0:T(8,128)(2,1)}), bf16[16,64,128]{2,1,0:T(8,128)(2,1)S(1)}, u32[]{:S(2)}, u32[]{:S(2)}) async-start(bf16[16,64,128]{2,1,0:T(8,128)(2,1)} %bitcast.4), calls=%async_computation.1 | async-start | bytes 524288 | tf_op jit(solution)/shard_map/all_to_all | solution.py:98
  23.5 0.8 copy.52
  24.4 9.0 %all-to-all-done.1 = bf16[16,64,128]{2,1,0:T(8,128)(2,1)S(1)} async-done(((bf16[16,64,128]{2,1,0:T(8,128)(2,1)}), bf16[16,64,128]{2,1,0:T(8,128)(2,1)S(1)}, u32[]{:S(2)}, u32[]{:S(2)}) %all-to-all-start.1) | async-done | bytes 262176 | tf_op jit(solution)/shard_map/all_to_all | solution.py:98
  33.4 3.5 %all-to-all-start.2 = ((bf16[16,64,128]{2,1,0:T(8,128)(2,1)}), bf16[16,64,128]{2,1,0:T(8,128)(2,1)S(1)}, u32[]{:S(2)}, u32[]{:S(2)}) async-start(bf16[16,64,128]{2,1,0:T(8,128)(2,1)} %bitcast.7), calls=%async_computation.2 | async-start | bytes 524288 | tf_op jit(solution)/shard_map/all_to_all | solution.py:100
  37.0 0.8 copy.55
  37.8 0.8 copy.53
  38.5 0.8 copy.54
  39.8 0.7 fusion.19
  40.5 6.5 %all-to-all-done.2 = bf16[16,64,128]{2,1,0:T(8,128)(2,1)S(1)} async-done(((bf16[16,64,128]{2,1,0:T(8,128)(2,1)}), bf16[16,64,128]{2,1,0:T(8,128)(2,1)S(1)}, u32[]{:S(2)}, u32[]{:S(2)}) %all-to-all-start.2) | async-done | bytes 262176 | tf_op jit(solution)/shard_map/all_to_all | solution.py:100
  47.0 3.5 %all-to-all-start.4 = ((bf16[16,64,128]{2,1,0:T(8,128)(2,1)}), bf16[16,64,128]{2,1,0:T(8,128)(2,1)S(1)}, u32[]{:S(2)}, u32[]{:S(2)}) async-start(bf16[16,64,128]{2,1,0:T(8,128)(2,1)} %bitcast.13), calls=%async_computation.4 | async-start | bytes 524288 | tf_op jit(solution)/shard_map/all_to_all | solution.py:102
  51.8 1.8 fusion.25
  53.6 6.9 %all-to-all-done.4 = bf16[16,64,128]{2,1,0:T(8,128)(2,1)S(1)} async-done(((bf16[16,64,128]{2,1,0:T(8,128)(2,1)}), bf16[16,64,128]{2,1,0:T(8,128)(2,1)S(1)}, u32[]{:S(2)}, u32[]{:S(2)}) %all-to-all-start.4) | async-done | bytes 262176 | tf_op jit(solution)/shard_map/all_to_all | solution.py:102
  60.5 3.5 %all-to-all-start.3 = ((bf16[16,64,128]{2,1,0:T(8,128)(2,1)}), bf16[16,64,128]{2,1,0:T(8,128)(2,1)S(1)}, u32[]{:S(2)}, u32[]{:S(2)}) async-start(bf16[16,64,128]{2,1,0:T(8,128)(2,1)} %bitcast.10), calls=%async_computation.3 | async-start | bytes 524288 | tf_op jit(solution)/shard_map/all_to_all | solution.py:101
  64.0 0.7 fusion.20
  65.3 8.7 %all-to-all-done.3 = bf16[16,64,128]{2,1,0:T(8,128)(2,1)S(1)} async-done(((bf16[16,64,128]{2,1,0:T(8,128)(2,1)}), bf16[16,64,128]{2,1,0:T(8,128)(2,1)S(1)}, u32[]{:S(2)}, u32[]{:S(2)}) %all-to-all-start.3) | async-done | bytes 262176 | tf_op jit(solution)/shard_map/all_to_all | solution.py:101
  74.0 3.7 %all-to-all-start.5 = ((bf16[16,64,128]{2,1,0:T(8,128)(2,1)}), bf16[16,64,128]{2,1,0:T(8,128)(2,1)S(1)}, u32[]{:S(2)}, u32[]{:S(2)}) async-start(bf16[16,64,128]{2,1,0:T(8,128)(2,1)} %bitcast.16), calls=%async_computation.5 | async-start | bytes 524288 | tf_op jit(solution)/shard_map/all_to_all | solution.py:99
  78.2 1.1 copy-done.8
  79.3 2.1 %multiply_reduce_fusion.2 = (f32[512]{0:T(512)S(1)}, f32[512,1024]{1,0:T(8,128)}) fusion(f32[512]{0:T(512)S(1)} %fusion.1, f32[512,1024]{1,0:T(8,128)S(1)} %get-tuple-element.85, f32[512]{0:T(512)S(1)} %get-tuple-element.84, f32[512,1024]{1,0:T(8,128)S(1)} %copy-done.8, bf16[512,128]{1,0:T(8,128)(2,1)S(1)} %bitcast.176, bf16[1024,128]{1,0:T(8,128)(2,1)S(1)} %bitcast.144), kind=kOutput, calls=%fused_computation.5 | convolution fusion | flops 137362944 | bytes 6690816 | tf_op jit(solution)/shard_map/dot_general | solution.py:10
  81.4 6.1 %all-to-all-done.5 = bf16[16,64,128]{2,1,0:T(8,128)(2,1)S(1)} async-done(((bf16[16,64,128]{2,1,0:T(8,128)(2,1)}), bf16[16,64,128]{2,1,0:T(8,128)(2,1)S(1)}, u32[]{:S(2)}, u32[]{:S(2)}) %all-to-all-start.5) | async-done | bytes 262176 | tf_op jit(solution)/shard_map/all_to_all | solution.py:99
  87.5 2.7 %multiply_reduce_fusion.1 = (f32[512]{0:T(512)S(1)}, f32[512]{0:T(512)S(1)}, f32[512,1024]{1,0:T(8,128)S(1)}) fusion(f32[512]{0:T(512)S(1)} %fusion.1, f32[512,1024]{1,0:T(8,128)S(1)} %get-tuple-element.85, f32[512]{0:T(512)S(1)} %get-tuple-element.84, f32[512,1024]{1,0:T(8,128)} %get-tuple-element.87, f32[512]{0:T(512)S(1)} %get-tuple-element.86, ...), kind=kOutput, calls=%fused_computation.3 | convolution fusion | flops 138411008 | bytes 6694912 | tf_op jit(solution)/shard_map/dot_general | solution.py:10
  90.3 1.2 multiply_convert_fusion
  91.6 1.1 fusion.26
  92.7 1.3 fusion.28
  97.3 1.3 multiply_convert_fusion.1
  98.7 1.0 fusion.27
  99.7 1.2 fusion.9
  101.8 2.2 %reduce.12 = bf16[1024,128]{1,0:T(8,128)(2,1)S(1)} reduce(bf16[1024,1,128]{2,1,0:T(2,128)(2,1)S(1)} %bitcast.149, bf16[]{:T(256)} %broadcast.116), dimensions={1}, to_apply=%bitcast.132.reduce_sub_computation | reduce | bytes 524290
  104.1 0.8 reshape.297
  104.8 3.8 %all-to-all-start.8 = ((bf16[16,2,4096]{2,1,0:T(2,128)(2,1)}), bf16[16,2,4096]{2,1,0:T(2,128)(2,1)S(1)}, u32[]{:S(2)}, u32[]{:S(2)}) async-start(bf16[16,2,4096]{2,1,0:T(2,128)(2,1)} %reshape.297), calls=%async_computation.8 | async-start | bytes 524288 | tf_op jit(solution)/shard_map/all_to_all | solution.py:115
  108.6 1.2 fusion.8
  109.9 1.2 multiply_reduce_fusion.6
  111.5 2.9 %reduce.13 = bf16[1024,128]{1,0:T(8,128)(2,1)} reduce(bf16[1024,1,128]{2,1,0:T(2,128)(2,1)S(1)} %bitcast.152, bf16[]{:T(256)} %broadcast.116), dimensions={1}, to_apply=%bitcast.133.reduce_sub_computation | reduce | bytes 524290
  114.4 1.7 reshape.295
  116.9 1.4 all-to-all-done.8
  118.4 4.3 %all-to-all-start.7 = ((bf16[16,2,4096]{2,1,0:T(2,128)(2,1)}), bf16[16,2,4096]{2,1,0:T(2,128)(2,1)S(1)}, u32[]{:S(2)}, u32[]{:S(2)}) async-start(bf16[16,2,4096]{2,1,0:T(2,128)(2,1)} %reshape.295), calls=%async_computation.7 | async-start | bytes 524288 | tf_op jit(solution)/shard_map/all_to_all | solution.py:114
  123.6 2.2 %reduce.11 = bf16[1024,128]{1,0:T(8,128)(2,1)S(1)} reduce(bf16[1024,1,128]{2,1,0:T(2,128)(2,1)S(1)} %bitcast.151, bf16[]{:T(256)} %broadcast.116), dimensions={1}, to_apply=%bitcast.134.reduce_sub_computation | reduce | bytes 524290
  125.8 0.8 reshape.293
  126.5 6.2 %all-to-all-done.7 = bf16[16,2,4096]{2,1,0:T(2,128)(2,1)S(1)} async-done(((bf16[16,2,4096]{2,1,0:T(2,128)(2,1)}), bf16[16,2,4096]{2,1,0:T(2,128)(2,1)S(1)}, u32[]{:S(2)}, u32[]{:S(2)}) %all-to-all-start.7) | async-done | bytes 262176 | tf_op jit(solution)/shard_map/all_to_all | solution.py:114
  132.7 3.5 %all-to-all-start.6 = ((bf16[16,2,4096]{2,1,0:T(2,128)(2,1)}), bf16[16,2,4096]{2,1,0:T(2,128)(2,1)S(1)}, u32[]{:S(2)}, u32[]{:S(2)}) async-start(bf16[16,2,4096]{2,1,0:T(2,128)(2,1)} %reshape.293), calls=%async_computation.6 | async-start | bytes 524288 | tf_op jit(solution)/shard_map/all_to_all | solution.py:113
  136.3 0.7 multiply_reduce_fusion.7
  138.5 40.5 %psum.7 = f32[2,16]{1,0:T(2,128)} all-reduce(f32[2,16]{1,0:T(2,128)S(1)} %and_select_fusion), channel_id=1, replica_groups=mesh['seq'=16,'dp'=2] {'seq','dp'}, use_global_device_ids=true, to_apply=%region_12.13 | all-reduce | flops 32 | bytes 256 | tf_op jit(solution)/shard_map/psum | solution.py:134
  180.0 0.8 copy.80
  180.8 0.9 copy_bitcast_fusion
  (103 shorter events, 10.6 us)
Async XLA Ops:
  0.6 9.3 %copy-start.21 = (bf16[2,64,1024]{2,1,0:T(8,128)(2,1)S(1)}, bf16[2,64,1024]{2,1,0:T(8,128)(2,1)}, u32[]{:S(2)}) copy-start(bf16[2,64,1024]{2,1,0:T(8,128)(2,1)} %param.19) | copy-start | bytes 786436
  0.6 10.1 %copy-start.22 = (bf16[2,64,1024]{2,1,0:T(8,128)(2,1)S(1)}, bf16[2,64,1024]{2,1,0:T(8,128)(2,1)}, u32[]{:S(2)}) copy-start(bf16[2,64,1024]{2,1,0:T(8,128)(2,1)} %param.20) | copy-start | bytes 786436
  0.7 10.2 %copy-start.23 = (bf16[2,64,1024]{2,1,0:T(8,128)(2,1)S(1)}, bf16[2,64,1024]{2,1,0:T(8,128)(2,1)}, u32[]{:S(2)}) copy-start(bf16[2,64,1024]{2,1,0:T(8,128)(2,1)} %param.21) | copy-start | bytes 786436
  2.5 17.4 %all-to-all-start = ((bf16[16,64,128]{2,1,0:T(8,128)(2,1)}), bf16[16,64,128]{2,1,0:T(8,128)(2,1)S(1)}, u32[]{:S(2)}, u32[]{:S(2)}) async-start(bf16[16,64,128]{2,1,0:T(8,128)(2,1)} %bitcast.1), calls=%async_computation | async-start | bytes 524288 | tf_op jit(solution)/shard_map/all_to_all | solution.py:97
  10.0 14.3 %copy-start.24 = (bf16[2,64,1024]{2,1,0:T(8,128)(2,1)S(1)}, bf16[2,64,1024]{2,1,0:T(8,128)(2,1)}, u32[]{:S(2)}) copy-start(bf16[2,64,1024]{2,1,0:T(8,128)(2,1)} %param.22) | copy-start | bytes 786436
  10.0 14.3 %copy-start.25 = (bf16[2,64,1024]{2,1,0:T(8,128)(2,1)S(1)}, bf16[2,64,1024]{2,1,0:T(8,128)(2,1)}, u32[]{:S(2)}) copy-start(bf16[2,64,1024]{2,1,0:T(8,128)(2,1)} %param.23) | copy-start | bytes 786436
  19.9 13.5 %all-to-all-start.1 = ((bf16[16,64,128]{2,1,0:T(8,128)(2,1)}), bf16[16,64,128]{2,1,0:T(8,128)(2,1)S(1)}, u32[]{:S(2)}, u32[]{:S(2)}) async-start(bf16[16,64,128]{2,1,0:T(8,128)(2,1)} %bitcast.4), calls=%async_computation.1 | async-start | bytes 524288 | tf_op jit(solution)/shard_map/all_to_all | solution.py:98
  33.4 13.5 %all-to-all-start.2 = ((bf16[16,64,128]{2,1,0:T(8,128)(2,1)}), bf16[16,64,128]{2,1,0:T(8,128)(2,1)S(1)}, u32[]{:S(2)}, u32[]{:S(2)}) async-start(bf16[16,64,128]{2,1,0:T(8,128)(2,1)} %bitcast.7), calls=%async_computation.2 | async-start | bytes 524288 | tf_op jit(solution)/shard_map/all_to_all | solution.py:100
  47.0 13.5 %copy-start.6 = (bf16[16,64,128]{2,1,0:T(8,128)(2,1)}, bf16[16,64,128]{2,1,0:T(8,128)(2,1)S(1)}, u32[]{:S(2)}) copy-start(bf16[16,64,128]{2,1,0:T(8,128)(2,1)S(1)} %all-to-all-done.2) | copy-start | bytes 786436
  47.0 13.5 %all-to-all-start.4 = ((bf16[16,64,128]{2,1,0:T(8,128)(2,1)}), bf16[16,64,128]{2,1,0:T(8,128)(2,1)S(1)}, u32[]{:S(2)}, u32[]{:S(2)}) async-start(bf16[16,64,128]{2,1,0:T(8,128)(2,1)} %bitcast.13), calls=%async_computation.4 | async-start | bytes 524288 | tf_op jit(solution)/shard_map/all_to_all | solution.py:102
  51.2 0.6 copy-start.13
  60.5 13.5 %all-to-all-start.3 = ((bf16[16,64,128]{2,1,0:T(8,128)(2,1)}), bf16[16,64,128]{2,1,0:T(8,128)(2,1)S(1)}, u32[]{:S(2)}, u32[]{:S(2)}) async-start(bf16[16,64,128]{2,1,0:T(8,128)(2,1)} %bitcast.10), calls=%async_computation.3 | async-start | bytes 524288 | tf_op jit(solution)/shard_map/all_to_all | solution.py:101
  64.7 22.8 %copy-start.26 = (bf16[8,64,128]{2,1,0:T(8,128)(2,1)}, bf16[8,64,128]{2,1,0:T(8,128)(2,1)S(1)}, u32[]{:S(2)}) copy-start(bf16[8,64,128]{2,1,0:T(8,128)(2,1)S(1)} %get-tuple-element.83) | copy-start | bytes 393220
  74.0 7.4 %copy-start.3 = (bf16[16,64,128]{2,1,0:T(8,128)(2,1)}, bf16[16,64,128]{2,1,0:T(8,128)(2,1)S(1)}, u32[]{:S(2)}) copy-start(bf16[16,64,128]{2,1,0:T(8,128)(2,1)S(1)} %all-to-all-done.3) | copy-start | bytes 786436
  74.0 13.5 %all-to-all-start.5 = ((bf16[16,64,128]{2,1,0:T(8,128)(2,1)}), bf16[16,64,128]{2,1,0:T(8,128)(2,1)S(1)}, u32[]{:S(2)}, u32[]{:S(2)}) async-start(bf16[16,64,128]{2,1,0:T(8,128)(2,1)} %bitcast.16), calls=%async_computation.5 | async-start | bytes 524288 | tf_op jit(solution)/shard_map/all_to_all | solution.py:99
  77.7 1.6 copy-start.8
  87.5 2.7 %copy-start.16 = (bf16[16,64,128]{2,1,0:T(8,128)(2,1)}, bf16[16,64,128]{2,1,0:T(8,128)(2,1)S(1)}, u32[]{:S(2)}) copy-start(bf16[16,64,128]{2,1,0:T(8,128)(2,1)S(1)} %all-to-all-done.5) | copy-start | bytes 786436
  87.5 2.7 %copy-start.10 = (f32[512,1024]{1,0:T(8,128)S(1)}, f32[512,1024]{1,0:T(8,128)}, u32[]{:S(2)}) copy-start(f32[512,1024]{1,0:T(8,128)} %get-tuple-element.87) | copy-start | bytes 6291460
  91.5 2.5 %copy-start.11 = (bf16[8,64,128]{2,1,0:T(8,128)(2,1)S(1)}, bf16[8,64,128]{2,1,0:T(8,128)(2,1)}, u32[]{:S(2)}) copy-start(bf16[8,64,128]{2,1,0:T(8,128)(2,1)} %get-tuple-element.78) | copy-start | bytes 393220
  91.5 2.8 %copy-start.20 = (bf16[8,64,128]{2,1,0:T(8,128)(2,1)S(1)}, bf16[8,64,128]{2,1,0:T(8,128)(2,1)}, u32[]{:S(2)}) copy-start(bf16[8,64,128]{2,1,0:T(8,128)(2,1)} %get-tuple-element.80) | copy-start | bytes 393220
  94.0 0.9 copy-start.4
  94.9 0.7 copy-start.18
  94.9 1.0 copy-start.28
  95.9 0.9 copy-start.17
  97.3 2.4 %copy-start.27 = (bf16[8,64,128]{2,1,0:T(8,128)(2,1)S(1)}, bf16[8,64,128]{2,1,0:T(8,128)(2,1)}, u32[]{:S(2)}) copy-start(bf16[8,64,128]{2,1,0:T(8,128)(2,1)} %copy-done.26) | copy-start | bytes 393220
  98.7 2.2 %copy-start = (bf16[512,512]{0,1:T(8,128)(2,1)}, bf16[512,512]{0,1:T(8,128)(2,1)S(1)}, u32[]{:S(2)}) copy-start(bf16[512,512]{0,1:T(8,128)(2,1)S(1)} %get-tuple-element.75) | copy-start | bytes 1572868
  100.9 7.7 %copy-start.2 = (bf16[512,512]{0,1:T(8,128)(2,1)S(1)}, bf16[512,512]{0,1:T(8,128)(2,1)}, u32[]{:S(2)}) copy-start(bf16[512,512]{0,1:T(8,128)(2,1)} %get-tuple-element.74) | copy-start | bytes 1572868
  100.9 7.7 %copy-start.12 = (bf16[8,64,128]{2,1,0:T(8,128)(2,1)S(1)}, bf16[8,64,128]{2,1,0:T(8,128)(2,1)}, u32[]{:S(2)}) copy-start(bf16[8,64,128]{2,1,0:T(8,128)(2,1)} %get-tuple-element.78) | copy-start | bytes 393220
  100.9 9.0 %copy-start.5 = (bf16[16,64,128]{2,1,0:T(8,128)(2,1)S(1)}, bf16[16,64,128]{2,1,0:T(8,128)(2,1)}, u32[]{:S(2)}) copy-start(bf16[16,64,128]{2,1,0:T(8,128)(2,1)} %copy-done.3) | copy-start | bytes 786436
  100.9 9.0 %copy-start.9 = (f32[1024,128]{1,0:T(8,128)S(1)}, f32[1024,128]{1,0:T(8,128)}, u32[]{:S(2)}) copy-start(f32[1024,128]{1,0:T(8,128)} %fusion.28) | copy-start | bytes 1572868
  100.9 9.0 %copy-start.14 = (bf16[8,64,128]{2,1,0:T(8,128)(2,1)S(1)}, bf16[8,64,128]{2,1,0:T(8,128)(2,1)}, u32[]{:S(2)}) copy-start(bf16[8,64,128]{2,1,0:T(8,128)(2,1)} %copy-done.13) | copy-start | bytes 393220
  104.8 13.5 %all-to-all-start.8 = ((bf16[16,2,4096]{2,1,0:T(2,128)(2,1)}), bf16[16,2,4096]{2,1,0:T(2,128)(2,1)S(1)}, u32[]{:S(2)}, u32[]{:S(2)}) async-start(bf16[16,2,4096]{2,1,0:T(2,128)(2,1)} %reshape.297), calls=%async_computation.8 | async-start | bytes 524288 | tf_op jit(solution)/shard_map/all_to_all | solution.py:115
  109.9 6.2 %copy-start.1 = (bf16[512,512]{0,1:T(8,128)(2,1)S(1)}, bf16[512,512]{0,1:T(8,128)(2,1)}, u32[]{:S(2)}) copy-start(bf16[512,512]{0,1:T(8,128)(2,1)} %copy-done) | copy-start | bytes 1572868
  111.1 5.4 %copy-start.15 = (f32[512,128]{1,0:T(8,128)S(1)}, f32[512,128]{1,0:T(8,128)}, u32[]{:S(2)}) copy-start(f32[512,128]{1,0:T(8,128)} %fusion.26) | copy-start | bytes 786436
  116.5 6.2 %copy-start.19 = (bf16[8,64,128]{2,1,0:T(8,128)(2,1)S(1)}, bf16[8,64,128]{2,1,0:T(8,128)(2,1)}, u32[]{:S(2)}) copy-start(bf16[8,64,128]{2,1,0:T(8,128)(2,1)} %copy-done.18) | copy-start | bytes 393220
  118.4 14.3 %all-to-all-start.7 = ((bf16[16,2,4096]{2,1,0:T(2,128)(2,1)}), bf16[16,2,4096]{2,1,0:T(2,128)(2,1)S(1)}, u32[]{:S(2)}, u32[]{:S(2)}) async-start(bf16[16,2,4096]{2,1,0:T(2,128)(2,1)} %reshape.295), calls=%async_computation.7 | async-start | bytes 524288 | tf_op jit(solution)/shard_map/all_to_all | solution.py:114
  123.1 13.2 %copy-start.7 = (bf16[16,64,128]{2,1,0:T(8,128)(2,1)S(1)}, bf16[16,64,128]{2,1,0:T(8,128)(2,1)}, u32[]{:S(2)}) copy-start(bf16[16,64,128]{2,1,0:T(8,128)(2,1)} %copy-done.6) | copy-start | bytes 786436
  123.1 15.3 %copy-start.29 = (pred[16]{0:T(512)(128)(4,1)S(1)}, pred[16]{0:T(512)(128)(4,1)}, u32[]{:S(2)}) copy-start(pred[16]{0:T(512)(128)(4,1)} %iota_compare_fusion.2) | copy-start | bytes 52
  132.7 47.0 %all-to-all-start.6 = ((bf16[16,2,4096]{2,1,0:T(2,128)(2,1)}), bf16[16,2,4096]{2,1,0:T(2,128)(2,1)S(1)}, u32[]{:S(2)}, u32[]{:S(2)}) async-start(bf16[16,2,4096]{2,1,0:T(2,128)(2,1)} %reshape.293), calls=%async_computation.6 | async-start | bytes 524288 | tf_op jit(solution)/shard_map/all_to_all | solution.py:113
where the time goes:
time: 183 us; the launch traced here: 182 us
  waiting for transfers between devices  53.8 us (29%)
  blocking collectives  40.5 us (22%)
  starting transfers between devices  36.8 us (20%)
  local copies, waits for them, and re-layouts  18.6 us (10%)
  matrix products  17.2 us (9%)
  other arithmetic  12 us (7%)
  between operations  2.68 us (1%)
    psum x1, blocking collectives, local(): curvature = lax.psum(board, ('seq', 'dp'))  40.5 us
    unnamed x76, local copies, waits for them, and re-layouts  9.05 us
    all_to_all x1, waiting for transfers between devices, local(): lax.all_to_all(to_items(queries), 'seq', split_axis=0, concat_axis=1, til...  9 us
    all_to_all x1, waiting for transfers between devices, local(): lax.all_to_all(to_items(key_rows), 'seq', split_axis=0, concat_axis=1, ti...  9 us
    all_to_all x1, waiting for transfers between devices, local(): lax.all_to_all(to_items(key_tangent), 'seq', split_axis=0, concat_axis=1,...  8.73 us
    dot_general x8, matrix products, inner_rows(): lax.dot_general(left, right, (((1,), (1,)), ((), ())), preferred_element_...  8.68 us
    all_to_all x1, starting transfers between devices, local(): lax.all_to_all(to_items(queries), 'seq', split_axis=0, concat_axis=1, til...  7.39 us
    unnamed x3, other arithmetic  7.33 us
  transfers between devices with their start and end apart: 9, of which 8 were waited for; matrix products, arithmetic and copies ran while one was open for 14% of the time, Pallas kernels for 0%

commit v1 on v0

--- a/solution.py
+++ b/solution.py
@@ -131,7 +131,8 @@
     head_here = lax.axis_index("dp") * local_heads + global_item % local_heads
     hit = jnp.logical_and(batch_index == batch_here, head_index == head_here)
     board = jnp.where(hit, kappas[item], 0.0)
-    curvature = lax.psum(board, ("seq", "dp"))
+    shards = lax.all_gather(board, ("seq", "dp"))
+    curvature = jnp.sum(shards, axis=0)
     return (outputs[0], outputs[1], outputs[2], curvature)
 
 

time: 183 us -> 212 us (1.16)
  blocking collectives: 40.5 us -> 68.7 us
    all_gather x0 -> x1, blocking collectives: none -> 68.7 us  [local(): shards = lax.all_gather(board, ('seq', 'dp'))]
    psum x1 -> x0, blocking collectives: 40.5 us -> none  [local(): curvature = lax.psum(board, ('seq', 'dp'))]
  transfers between devices with their start and end apart: 9 -> 9, of which waited for: 8 -> 8; matrix products, arithmetic and copies ran while one was open for 14% -> 12% of each run, Pallas kernels for 0% -> 0%
where the time goes in v1:
time: 212 us; the launch traced here: 210 us
  blocking collectives  68.7 us (32%)
  waiting for transfers between devices  53.8 us (25%)
  starting transfers between devices  36.8 us (17%)
  local copies, waits for them, and re-layouts  18.6 us (9%)
  matrix products  17.2 us (8%)
  other arithmetic  12.6 us (6%)
  between operations  2.68 us (1%)
    all_gather x1, blocking collectives, local(): shards = lax.all_gather(board, ('seq', 'dp'))  68.7 us
    unnamed x76, local copies, waits for them, and re-layouts  9.05 us
    all_to_all x1, waiting for transfers between devices, local(): lax.all_to_all(to_items(queries), 'seq', split_axis=0, concat_axis=1, til...  9 us
    all_to_all x1, waiting for transfers between devices, local(): lax.all_to_all(to_items(key_rows), 'seq', split_axis=0, concat_axis=1, ti...  9 us
    all_to_all x1, waiting for transfers between devices, local(): lax.all_to_all(to_items(key_tangent), 'seq', split_axis=0, concat_axis=1,...  8.73 us
    dot_general x8, matrix products, inner_rows(): lax.dot_general(left, right, (((1,), (1,)), ((), ())), preferred_element_...  8.68 us
    all_to_all x1, starting transfers between devices, local(): lax.all_to_all(to_items(queries), 'seq', split_axis=0, concat_axis=1, til...  7.39 us
    unnamed x3, other arithmetic  7.33 us
  transfers between devices with their start and end apart: 9, of which 8 were waited for; matrix products, arithmetic and copies ran while one was open for 12% of the time, Pallas kernels for 0%

profile of v1, /device:TPU:0, one launch (start us, length us, event | category | flops | bytes accessed | tf_op | source)
XLA Modules:
  0.0 210.4 jit_solution(11657384715683602550)
XLA Ops:
  0.7 1.1 copy.68
  1.8 0.8 copy.50
  2.5 7.4 %all-to-all-start = ((bf16[16,64,128]{2,1,0:T(8,128)(2,1)}), bf16[16,64,128]{2,1,0:T(8,128)(2,1)S(1)}, u32[]{:S(2)}, u32[]{:S(2)}) async-start(bf16[16,64,128]{2,1,0:T(8,128)(2,1)} %bitcast.1), calls=%async_computation | async-start | bytes 524288 | tf_op jit(solution)/shard_map/all_to_all | solution.py:97
  10.0 0.8 copy.51
  10.9 9.0 %all-to-all-done = bf16[16,64,128]{2,1,0:T(8,128)(2,1)S(1)} async-done(((bf16[16,64,128]{2,1,0:T(8,128)(2,1)}), bf16[16,64,128]{2,1,0:T(8,128)(2,1)S(1)}, u32[]{:S(2)}, u32[]{:S(2)}) %all-to-all-start) | async-done | bytes 262176 | tf_op jit(solution)/shard_map/all_to_all | solution.py:97
  19.9 3.5 %all-to-all-start.1 = ((bf16[16,64,128]{2,1,0:T(8,128)(2,1)}), bf16[16,64,128]{2,1,0:T(8,128)(2,1)S(1)}, u32[]{:S(2)}, u32[]{:S(2)}) async-start(bf16[16,64,128]{2,1,0:T(8,128)(2,1)} %bitcast.4), calls=%async_computation.1 | async-start | bytes 524288 | tf_op jit(solution)/shard_map/all_to_all | solution.py:98
  23.5 0.8 copy.52
  24.4 9.0 %all-to-all-done.1 = bf16[16,64,128]{2,1,0:T(8,128)(2,1)S(1)} async-done(((bf16[16,64,128]{2,1,0:T(8,128)(2,1)}), bf16[16,64,128]{2,1,0:T(8,128)(2,1)S(1)}, u32[]{:S(2)}, u32[]{:S(2)}) %all-to-all-start.1) | async-done | bytes 262176 | tf_op jit(solution)/shard_map/all_to_all | solution.py:98
  33.4 3.5 %all-to-all-start.2 = ((bf16[16,64,128]{2,1,0:T(8,128)(2,1)}), bf16[16,64,128]{2,1,0:T(8,128)(2,1)S(1)}, u32[]{:S(2)}, u32[]{:S(2)}) async-start(bf16[16,64,128]{2,1,0:T(8,128)(2,1)} %bitcast.7), calls=%async_computation.2 | async-start | bytes 524288 | tf_op jit(solution)/shard_map/all_to_all | solution.py:100
  37.0 0.8 copy.55
  37.8 0.8 copy.53
  38.5 0.8 copy.54
  39.8 0.7 fusion.19
  40.5 6.5 %all-to-all-done.2 = bf16[16,64,128]{2,1,0:T(8,128)(2,1)S(1)} async-done(((bf16[16,64,128]{2,1,0:T(8,128)(2,1)}), bf16[16,64,128]{2,1,0:T(8,128)(2,1)S(1)}, u32[]{:S(2)}, u32[]{:S(2)}) %all-to-all-start.2) | async-done | bytes 262176 | tf_op jit(solution)/shard_map/all_to_all | solution.py:100
  47.0 3.5 %all-to-all-start.4 = ((bf16[16,64,128]{2,1,0:T(8,128)(2,1)}), bf16[16,64,128]{2,1,0:T(8,128)(2,1)S(1)}, u32[]{:S(2)}, u32[]{:S(2)}) async-start(bf16[16,64,128]{2,1,0:T(8,128)(2,1)} %bitcast.13), calls=%async_computation.4 | async-start | bytes 524288 | tf_op jit(solution)/shard_map/all_to_all | solution.py:102
  51.8 1.8 fusion.25
  53.6 6.9 %all-to-all-done.4 = bf16[16,64,128]{2,1,0:T(8,128)(2,1)S(1)} async-done(((bf16[16,64,128]{2,1,0:T(8,128)(2,1)}), bf16[16,64,128]{2,1,0:T(8,128)(2,1)S(1)}, u32[]{:S(2)}, u32[]{:S(2)}) %all-to-all-start.4) | async-done | bytes 262176 | tf_op jit(solution)/shard_map/all_to_all | solution.py:102
  60.5 3.5 %all-to-all-start.3 = ((bf16[16,64,128]{2,1,0:T(8,128)(2,1)}), bf16[16,64,128]{2,1,0:T(8,128)(2,1)S(1)}, u32[]{:S(2)}, u32[]{:S(2)}) async-start(bf16[16,64,128]{2,1,0:T(8,128)(2,1)} %bitcast.10), calls=%async_computation.3 | async-start | bytes 524288 | tf_op jit(solution)/shard_map/all_to_all | solution.py:101
  64.0 0.7 fusion.20
  65.3 8.7 %all-to-all-done.3 = bf16[16,64,128]{2,1,0:T(8,128)(2,1)S(1)} async-done(((bf16[16,64,128]{2,1,0:T(8,128)(2,1)}), bf16[16,64,128]{2,1,0:T(8,128)(2,1)S(1)}, u32[]{:S(2)}, u32[]{:S(2)}) %all-to-all-start.3) | async-done | bytes 262176 | tf_op jit(solution)/shard_map/all_to_all | solution.py:101
  74.0 3.7 %all-to-all-start.5 = ((bf16[16,64,128]{2,1,0:T(8,128)(2,1)}), bf16[16,64,128]{2,1,0:T(8,128)(2,1)S(1)}, u32[]{:S(2)}, u32[]{:S(2)}) async-start(bf16[16,64,128]{2,1,0:T(8,128)(2,1)} %bitcast.16), calls=%async_computation.5 | async-start | bytes 524288 | tf_op jit(solution)/shard_map/all_to_all | solution.py:99
  78.2 1.1 copy-done.8
  79.3 2.1 %multiply_reduce_fusion.2 = (f32[512]{0:T(512)S(1)}, f32[512,1024]{1,0:T(8,128)}) fusion(f32[512]{0:T(512)S(1)} %fusion.1, f32[512,1024]{1,0:T(8,128)S(1)} %get-tuple-element.85, f32[512]{0:T(512)S(1)} %get-tuple-element.84, f32[512,1024]{1,0:T(8,128)S(1)} %copy-done.8, bf16[512,128]{1,0:T(8,128)(2,1)S(1)} %bitcast.176, bf16[1024,128]{1,0:T(8,128)(2,1)S(1)} %bitcast.144), kind=kOutput, calls=%fused_computation.5 | convolution fusion | flops 137362944 | bytes 6690816 | tf_op jit(solution)/shard_map/dot_general | solution.py:10
  81.4 6.1 %all-to-all-done.5 = bf16[16,64,128]{2,1,0:T(8,128)(2,1)S(1)} async-done(((bf16[16,64,128]{2,1,0:T(8,128)(2,1)}), bf16[16,64,128]{2,1,0:T(8,128)(2,1)S(1)}, u32[]{:S(2)}, u32[]{:S(2)}) %all-to-all-start.5) | async-done | bytes 262176 | tf_op jit(solution)/shard_map/all_to_all | solution.py:99
  87.5 2.7 %multiply_reduce_fusion.1 = (f32[512]{0:T(512)S(1)}, f32[512]{0:T(512)S(1)}, f32[512,1024]{1,0:T(8,128)S(1)}) fusion(f32[512]{0:T(512)S(1)} %fusion.1, f32[512,1024]{1,0:T(8,128)S(1)} %get-tuple-element.85, f32[512]{0:T(512)S(1)} %get-tuple-element.84, f32[512,1024]{1,0:T(8,128)} %get-tuple-element.87, f32[512]{0:T(512)S(1)} %get-tuple-element.86, ...), kind=kOutput, calls=%fused_computation.3 | convolution fusion | flops 138411008 | bytes 6694912 | tf_op jit(solution)/shard_map/dot_general | solution.py:10
  90.3 1.2 multiply_convert_fusion
  91.6 1.1 fusion.26
  92.7 1.3 fusion.28
  97.3 1.3 multiply_convert_fusion.1
  98.7 1.0 fusion.27
  99.7 1.2 fusion.9
  101.8 2.2 %reduce.12 = bf16[1024,128]{1,0:T(8,128)(2,1)S(1)} reduce(bf16[1024,1,128]{2,1,0:T(2,128)(2,1)S(1)} %bitcast.149, bf16[]{:T(256)} %broadcast.167), dimensions={1}, to_apply=%bitcast.132.reduce_sub_computation | reduce | bytes 524290
  104.1 0.8 reshape.343
  104.8 3.8 %all-to-all-start.8 = ((bf16[16,2,4096]{2,1,0:T(2,128)(2,1)}), bf16[16,2,4096]{2,1,0:T(2,128)(2,1)S(1)}, u32[]{:S(2)}, u32[]{:S(2)}) async-start(bf16[16,2,4096]{2,1,0:T(2,128)(2,1)} %reshape.343), calls=%async_computation.8 | async-start | bytes 524288 | tf_op jit(solution)/shard_map/all_to_all | solution.py:115
  108.6 1.2 fusion.8
  109.9 1.2 multiply_reduce_fusion.6
  111.5 2.9 %reduce.13 = bf16[1024,128]{1,0:T(8,128)(2,1)} reduce(bf16[1024,1,128]{2,1,0:T(2,128)(2,1)S(1)} %bitcast.152, bf16[]{:T(256)} %broadcast.167), dimensions={1}, to_apply=%bitcast.133.reduce_sub_computation | reduce | bytes 524290
  114.4 1.7 reshape.341
  116.9 1.4 all-to-all-done.8
  118.4 4.3 %all-to-all-start.7 = ((bf16[16,2,4096]{2,1,0:T(2,128)(2,1)}), bf16[16,2,4096]{2,1,0:T(2,128)(2,1)S(1)}, u32[]{:S(2)}, u32[]{:S(2)}) async-start(bf16[16,2,4096]{2,1,0:T(2,128)(2,1)} %reshape.341), calls=%async_computation.7 | async-start | bytes 524288 | tf_op jit(solution)/shard_map/all_to_all | solution.py:114
  123.6 2.2 %reduce.11 = bf16[1024,128]{1,0:T(8,128)(2,1)S(1)} reduce(bf16[1024,1,128]{2,1,0:T(2,128)(2,1)S(1)} %bitcast.151, bf16[]{:T(256)} %broadcast.167), dimensions={1}, to_apply=%bitcast.134.reduce_sub_computation | reduce | bytes 524290
  125.8 0.8 reshape.339
  126.5 6.2 %all-to-all-done.7 = bf16[16,2,4096]{2,1,0:T(2,128)(2,1)S(1)} async-done(((bf16[16,2,4096]{2,1,0:T(2,128)(2,1)}), bf16[16,2,4096]{2,1,0:T(2,128)(2,1)S(1)}, u32[]{:S(2)}, u32[]{:S(2)}) %all-to-all-start.7) | async-done | bytes 262176 | tf_op jit(solution)/shard_map/all_to_all | solution.py:114
  132.7 3.5 %all-to-all-start.6 = ((bf16[16,2,4096]{2,1,0:T(2,128)(2,1)}), bf16[16,2,4096]{2,1,0:T(2,128)(2,1)S(1)}, u32[]{:S(2)}, u32[]{:S(2)}) async-start(bf16[16,2,4096]{2,1,0:T(2,128)(2,1)} %reshape.339), calls=%async_computation.6 | async-start | bytes 524288 | tf_op jit(solution)/shard_map/all_to_all | solution.py:113
  136.3 0.7 multiply_reduce_fusion.7
  138.5 68.7 %all_gather.4 = f32[32,2,16]{2,1,0:T(2,128)S(1)} all-gather(f32[1,2,16]{2,1,0:T(2,128)S(1)} %and_select_fusion), channel_id=1, replica_groups=mesh['seq'=16,'dp'=2] {'seq','dp'}, dimensions={0}, use_global_device_ids=true | all-gather | bytes 4224 | tf_op jit(solution)/shard_map/all_gather | solution.py:134
  208.8 0.8 copy.80
  209.5 0.9 copy_bitcast_fusion
  (104 shorter events, 11.2 us)
Async XLA Ops:
  0.6 9.3 %copy-start.21 = (bf16[2,64,1024]{2,1,0:T(8,128)(2,1)S(1)}, bf16[2,64,1024]{2,1,0:T(8,128)(2,1)}, u32[]{:S(2)}) copy-start(bf16[2,64,1024]{2,1,0:T(8,128)(2,1)} %param.19) | copy-start | bytes 786436
  0.6 10.1 %copy-start.22 = (bf16[2,64,1024]{2,1,0:T(8,128)(2,1)S(1)}, bf16[2,64,1024]{2,1,0:T(8,128)(2,1)}, u32[]{:S(2)}) copy-start(bf16[2,64,1024]{2,1,0:T(8,128)(2,1)} %param.20) | copy-start | bytes 786436
  0.7 10.2 %copy-start.23 = (bf16[2,64,1024]{2,1,0:T(8,128)(2,1)S(1)}, bf16[2,64,1024]{2,1,0:T(8,128)(2,1)}, u32[]{:S(2)}) copy-start(bf16[2,64,1024]{2,1,0:T(8,128)(2,1)} %param.21) | copy-start | bytes 786436
  2.5 17.4 %all-to-all-start = ((bf16[16,64,128]{2,1,0:T(8,128)(2,1)}), bf16[16,64,128]{2,1,0:T(8,128)(2,1)S(1)}, u32[]{:S(2)}, u32[]{:S(2)}) async-start(bf16[16,64,128]{2,1,0:T(8,128)(2,1)} %bitcast.1), calls=%async_computation | async-start | bytes 524288 | tf_op jit(solution)/shard_map/all_to_all | solution.py:97
  10.0 14.3 %copy-start.24 = (bf16[2,64,1024]{2,1,0:T(8,128)(2,1)S(1)}, bf16[2,64,1024]{2,1,0:T(8,128)(2,1)}, u32[]{:S(2)}) copy-start(bf16[2,64,1024]{2,1,0:T(8,128)(2,1)} %param.22) | copy-start | bytes 786436
  10.0 14.3 %copy-start.25 = (bf16[2,64,1024]{2,1,0:T(8,128)(2,1)S(1)}, bf16[2,64,1024]{2,1,0:T(8,128)(2,1)}, u32[]{:S(2)}) copy-start(bf16[2,64,1024]{2,1,0:T(8,128)(2,1)} %param.23) | copy-start | bytes 786436
  19.9 13.5 %all-to-all-start.1 = ((bf16[16,64,128]{2,1,0:T(8,128)(2,1)}), bf16[16,64,128]{2,1,0:T(8,128)(2,1)S(1)}, u32[]{:S(2)}, u32[]{:S(2)}) async-start(bf16[16,64,128]{2,1,0:T(8,128)(2,1)} %bitcast.4), calls=%async_computation.1 | async-start | bytes 524288 | tf_op jit(solution)/shard_map/all_to_all | solution.py:98
  33.4 13.5 %all-to-all-start.2 = ((bf16[16,64,128]{2,1,0:T(8,128)(2,1)}), bf16[16,64,128]{2,1,0:T(8,128)(2,1)S(1)}, u32[]{:S(2)}, u32[]{:S(2)}) async-start(bf16[16,64,128]{2,1,0:T(8,128)(2,1)} %bitcast.7), calls=%async_computation.2 | async-start | bytes 524288 | tf_op jit(solution)/shard_map/all_to_all | solution.py:100
  47.0 13.5 %copy-start.6 = (bf16[16,64,128]{2,1,0:T(8,128)(2,1)}, bf16[16,64,128]{2,1,0:T(8,128)(2,1)S(1)}, u32[]{:S(2)}) copy-start(bf16[16,64,128]{2,1,0:T(8,128)(2,1)S(1)} %all-to-all-done.2) | copy-start | bytes 786436
  47.0 13.5 %all-to-all-start.4 = ((bf16[16,64,128]{2,1,0:T(8,128)(2,1)}), bf16[16,64,128]{2,1,0:T(8,128)(2,1)S(1)}, u32[]{:S(2)}, u32[]{:S(2)}) async-start(bf16[16,64,128]{2,1,0:T(8,128)(2,1)} %bitcast.13), calls=%async_computation.4 | async-start | bytes 524288 | tf_op jit(solution)/shard_map/all_to_all | solution.py:102
  51.2 0.6 copy-start.13
  60.5 13.5 %all-to-all-start.3 = ((bf16[16,64,128]{2,1,0:T(8,128)(2,1)}), bf16[16,64,128]{2,1,0:T(8,128)(2,1)S(1)}, u32[]{:S(2)}, u32[]{:S(2)}) async-start(bf16[16,64,128]{2,1,0:T(8,128)(2,1)} %bitcast.10), calls=%async_computation.3 | async-start | bytes 524288 | tf_op jit(solution)/shard_map/all_to_all | solution.py:101
  64.7 22.8 %copy-start.26 = (bf16[8,64,128]{2,1,0:T(8,128)(2,1)}, bf16[8,64,128]{2,1,0:T(8,128)(2,1)S(1)}, u32[]{:S(2)}) copy-start(bf16[8,64,128]{2,1,0:T(8,128)(2,1)S(1)} %get-tuple-element.83) | copy-start | bytes 393220
  74.0 7.4 %copy-start.3 = (bf16[16,64,128]{2,1,0:T(8,128)(2,1)}, bf16[16,64,128]{2,1,0:T(8,128)(2,1)S(1)}, u32[]{:S(2)}) copy-start(bf16[16,64,128]{2,1,0:T(8,128)(2,1)S(1)} %all-to-all-done.3) | copy-start | bytes 786436
  74.0 13.5 %all-to-all-start.5 = ((bf16[16,64,128]{2,1,0:T(8,128)(2,1)}), bf16[16,64,128]{2,1,0:T(8,128)(2,1)S(1)}, u32[]{:S(2)}, u32[]{:S(2)}) async-start(bf16[16,64,128]{2,1,0:T(8,128)(2,1)} %bitcast.16), calls=%async_computation.5 | async-start | bytes 524288 | tf_op jit(solution)/shard_map/all_to_all | solution.py:99
  77.7 1.6 copy-start.8
  87.5 2.7 %copy-start.16 = (bf16[16,64,128]{2,1,0:T(8,128)(2,1)}, bf16[16,64,128]{2,1,0:T(8,128)(2,1)S(1)}, u32[]{:S(2)}) copy-start(bf16[16,64,128]{2,1,0:T(8,128)(2,1)S(1)} %all-to-all-done.5) | copy-start | bytes 786436
  87.5 2.7 %copy-start.10 = (f32[512,1024]{1,0:T(8,128)S(1)}, f32[512,1024]{1,0:T(8,128)}, u32[]{:S(2)}) copy-start(f32[512,1024]{1,0:T(8,128)} %get-tuple-element.87) | copy-start | bytes 6291460
  91.5 2.5 %copy-start.11 = (bf16[8,64,128]{2,1,0:T(8,128)(2,1)S(1)}, bf16[8,64,128]{2,1,0:T(8,128)(2,1)}, u32[]{:S(2)}) copy-start(bf16[8,64,128]{2,1,0:T(8,128)(2,1)} %get-tuple-element.78) | copy-start | bytes 393220
  91.5 2.8 %copy-start.20 = (bf16[8,64,128]{2,1,0:T(8,128)(2,1)S(1)}, bf16[8,64,128]{2,1,0:T(8,128)(2,1)}, u32[]{:S(2)}) copy-start(bf16[8,64,128]{2,1,0:T(8,128)(2,1)} %get-tuple-element.80) | copy-start | bytes 393220
  94.0 0.9 copy-start.4
  94.9 0.7 copy-start.18
  94.9 1.0 copy-start.28
  95.9 0.9 copy-start.17
  97.3 2.4 %copy-start.27 = (bf16[8,64,128]{2,1,0:T(8,128)(2,1)S(1)}, bf16[8,64,128]{2,1,0:T(8,128)(2,1)}, u32[]{:S(2)}) copy-start(bf16[8,64,128]{2,1,0:T(8,128)(2,1)} %copy-done.26) | copy-start | bytes 393220
  98.7 2.2 %copy-start = (bf16[512,512]{0,1:T(8,128)(2,1)}, bf16[512,512]{0,1:T(8,128)(2,1)S(1)}, u32[]{:S(2)}) copy-start(bf16[512,512]{0,1:T(8,128)(2,1)S(1)} %get-tuple-element.75) | copy-start | bytes 1572868
  100.9 7.7 %copy-start.2 = (bf16[512,512]{0,1:T(8,128)(2,1)S(1)}, bf16[512,512]{0,1:T(8,128)(2,1)}, u32[]{:S(2)}) copy-start(bf16[512,512]{0,1:T(8,128)(2,1)} %get-tuple-element.74) | copy-start | bytes 1572868
  100.9 7.7 %copy-start.12 = (bf16[8,64,128]{2,1,0:T(8,128)(2,1)S(1)}, bf16[8,64,128]{2,1,0:T(8,128)(2,1)}, u32[]{:S(2)}) copy-start(bf16[8,64,128]{2,1,0:T(8,128)(2,1)} %get-tuple-element.78) | copy-start | bytes 393220
  100.9 9.0 %copy-start.5 = (bf16[16,64,128]{2,1,0:T(8,128)(2,1)S(1)}, bf16[16,64,128]{2,1,0:T(8,128)(2,1)}, u32[]{:S(2)}) copy-start(bf16[16,64,128]{2,1,0:T(8,128)(2,1)} %copy-done.3) | copy-start | bytes 786436
  100.9 9.0 %copy-start.9 = (f32[1024,128]{1,0:T(8,128)S(1)}, f32[1024,128]{1,0:T(8,128)}, u32[]{:S(2)}) copy-start(f32[1024,128]{1,0:T(8,128)} %fusion.28) | copy-start | bytes 1572868
  100.9 9.0 %copy-start.14 = (bf16[8,64,128]{2,1,0:T(8,128)(2,1)S(1)}, bf16[8,64,128]{2,1,0:T(8,128)(2,1)}, u32[]{:S(2)}) copy-start(bf16[8,64,128]{2,1,0:T(8,128)(2,1)} %copy-done.13) | copy-start | bytes 393220
  104.8 13.5 %all-to-all-start.8 = ((bf16[16,2,4096]{2,1,0:T(2,128)(2,1)}), bf16[16,2,4096]{2,1,0:T(2,128)(2,1)S(1)}, u32[]{:S(2)}, u32[]{:S(2)}) async-start(bf16[16,2,4096]{2,1,0:T(2,128)(2,1)} %reshape.343), calls=%async_computation.8 | async-start | bytes 524288 | tf_op jit(solution)/shard_map/all_to_all | solution.py:115
  109.9 6.2 %copy-start.1 = (bf16[512,512]{0,1:T(8,128)(2,1)S(1)}, bf16[512,512]{0,1:T(8,128)(2,1)}, u32[]{:S(2)}) copy-start(bf16[512,512]{0,1:T(8,128)(2,1)} %copy-done) | copy-start | bytes 1572868
  111.1 5.4 %copy-start.15 = (f32[512,128]{1,0:T(8,128)S(1)}, f32[512,128]{1,0:T(8,128)}, u32[]{:S(2)}) copy-start(f32[512,128]{1,0:T(8,128)} %fusion.26) | copy-start | bytes 786436
  116.5 6.2 %copy-start.19 = (bf16[8,64,128]{2,1,0:T(8,128)(2,1)S(1)}, bf16[8,64,128]{2,1,0:T(8,128)(2,1)}, u32[]{:S(2)}) copy-start(bf16[8,64,128]{2,1,0:T(8,128)(2,1)} %copy-done.18) | copy-start | bytes 393220
  118.4 14.3 %all-to-all-start.7 = ((bf16[16,2,4096]{2,1,0:T(2,128)(2,1)}), bf16[16,2,4096]{2,1,0:T(2,128)(2,1)S(1)}, u32[]{:S(2)}, u32[]{:S(2)}) async-start(bf16[16,2,4096]{2,1,0:T(2,128)(2,1)} %reshape.341), calls=%async_computation.7 | async-start | bytes 524288 | tf_op jit(solution)/shard_map/all_to_all | solution.py:114
  123.1 13.2 %copy-start.7 = (bf16[16,64,128]{2,1,0:T(8,128)(2,1)S(1)}, bf16[16,64,128]{2,1,0:T(8,128)(2,1)}, u32[]{:S(2)}) copy-start(bf16[16,64,128]{2,1,0:T(8,128)(2,1)} %copy-done.6) | copy-start | bytes 786436
  123.1 15.3 %copy-start.29 = (pred[16]{0:T(512)(128)(4,1)S(1)}, pred[16]{0:T(512)(128)(4,1)}, u32[]{:S(2)}) copy-start(pred[16]{0:T(512)(128)(4,1)} %iota_compare_fusion.2) | copy-start | bytes 52
  132.7 75.7 %all-to-all-start.6 = ((bf16[16,2,4096]{2,1,0:T(2,128)(2,1)}), bf16[16,2,4096]{2,1,0:T(2,128)(2,1)S(1)}, u32[]{:S(2)}, u32[]{:S(2)}) async-start(bf16[16,2,4096]{2,1,0:T(2,128)(2,1)} %reshape.339), calls=%async_computation.6 | async-start | bytes 524288 | tf_op jit(solution)/shard_map/all_to_all | solution.py:113
